TPU v7x, 128 devices: a whole 4x4x4 slice. The times are simulated.
128 devices in a mesh: req: 16 (over y, z), tp: 8 (over x, core).
Axes of the slice: x: 4, y: 4, z: 4, core: 2. Of those that a mesh axis runs over, the one named last changes fastest.
Arguments:
- short_tokens: bfloat16 [1536, 3072], P('req')
- long_tokens: bfloat16 [8, 3072], replicated
- norm_gain: bfloat16 [3072], replicated, may hold values from 0.5 to 1.5
- w_query: bfloat16 [3072, 3072], P(None, 'tp'), may hold values from -0.109375 to 0.109375
- w_key: bfloat16 [3072, 1024], P(None, 'tp'), may hold values from -0.109375 to 0.109375
- w_value: bfloat16 [3072, 1024], P(None, 'tp'), may hold values from -0.109375 to 0.109375
- w_out: bfloat16 [3072, 3072], P('tp'), may hold values from -0.109375 to 0.109375
- short_lengths: int32 [1536], P('req'), may hold values from 0 to 127
- long_lengths: int32 [8], replicated, may hold values from 6144 to 8191
- short_cache: bfloat16 [1536, 8, 128, 256], P('req', 'tp'), may hold values from -120 to 120
- long_cache: bfloat16 [8, 8, 8192, 256], P(None, 'tp', 'req'), may hold values from -120 to 120
Outputs:
- short_hidden: bfloat16 [1536, 3072], P('req')
- long_hidden: bfloat16 [8, 3072], replicated
- short_cache_new: bfloat16 [1536, 8, 128, 256], P('req', 'tp')
- long_cache_new: bfloat16 [8, 8, 8192, 256], P(None, 'tp', 'req')
All inputs are finite; a program needn't handle non-finite values.
Results may differ from a plain program's by a relative error of at most 0.0095.
Values may be sent and summed in bfloat16 or wider, within the bound.
A program may use at most 128 MiB of HBM per device.

v0:
```python
import jax
import jax.numpy as jnp
from jax import lax
from jax.sharding import PartitionSpec as P

rope_theta = 500000.0
floor_score = -1e30


def merged(value, axis, join):
    pieces = jax.tree.map(lambda part: lax.all_gather(part, axis), value)
    head = jax.tree.map(lambda part: part[0], pieces)
    tail = jax.tree.map(lambda part: part[1:], pieces)
    total, _ = lax.scan(lambda total, slab: (join(total, slab), None), head, tail)
    return total


def rotate(values, positions):
    half = values.shape[-1] // 2
    freq = rope_theta ** (-(jnp.arange(half, dtype=jnp.float32) * 2.0 / values.shape[-1]))
    angle = positions.astype(jnp.float32)[:, None] * freq[None, :]
    cosine = jnp.cos(angle)[:, None, :]
    sine = jnp.sin(angle)[:, None, :]
    front = values[..., :half]
    back = values[..., half:]
    return jnp.concatenate([front * cosine - back * sine, back * cosine + front * sine], axis=-1)


def join_partials(earlier, later):
    peak_one, total_one, summed_one = earlier
    peak_two, total_two, summed_two = later
    peak_new = jnp.maximum(peak_one, peak_two)
    factor_one = jnp.exp(peak_one - peak_new)
    factor_two = jnp.exp(peak_two - peak_new)
    total_new = total_one * factor_one + total_two * factor_two
    summed_new = summed_one * factor_one[..., None] + summed_two * factor_two[..., None]
    return (peak_new, total_new, summed_new)


def per_device(
    short_tokens,
    long_tokens,
    norm_gain,
    w_query,
    w_key,
    w_value,
    w_out,
    short_lengths,
    long_lengths,
    short_cache,
    long_cache,
):
    head_size = short_cache.shape[-1] // 2
    kv_local = short_cache.shape[1]
    short_count = short_tokens.shape[0]
    long_count = long_tokens.shape[0]
    all_tokens = jnp.concatenate([short_tokens, long_tokens], axis=0)
    positions = jnp.concatenate([short_lengths, long_lengths], axis=0)
    total_rows = all_tokens.shape[0]
    residual = all_tokens.astype(jnp.float32)
    normed = (
        residual
        * lax.rsqrt(jnp.mean(residual * residual, axis=-1, keepdims=True) + 1e-05)
        * norm_gain.astype(jnp.float32)
    ).astype(jnp.bfloat16)
    query = jnp.dot(normed, w_query, preferred_element_type=jnp.float32).reshape(
        total_rows, -1, head_size
    )
    group_size = query.shape[1] // kv_local
    query = (
        rotate(query, positions)
        .astype(jnp.bfloat16)
        .reshape(total_rows, kv_local, group_size, head_size)
    )
    key_new = jnp.dot(normed, w_key, preferred_element_type=jnp.float32).reshape(
        total_rows, kv_local, head_size
    )
    key_new = rotate(key_new, positions).astype(jnp.bfloat16)
    value_new = (
        jnp.dot(normed, w_value, preferred_element_type=jnp.float32)
        .reshape(total_rows, kv_local, head_size)
        .astype(jnp.bfloat16)
    )
    fresh = jnp.concatenate([key_new, value_new], axis=-1)
    score_scale = 1.0 / jnp.sqrt(jnp.float32(head_size))
    short_slots = jnp.arange(short_cache.shape[2], dtype=jnp.int32)
    short_write = short_slots[None, :] == short_lengths[:, None]
    short_out = jnp.where(
        short_write[:, None, :, None], fresh[:short_count, :, None, :], short_cache
    )
    short_scores = (
        jnp.einsum(
            "rkgd,rksd->rkgs",
            query[:short_count],
            short_out[..., :head_size],
            preferred_element_type=jnp.float32,
        )
        * score_scale
    )
    short_valid = (short_slots[None, :] <= short_lengths[:, None])[:, None, None, :]
    short_scores = jnp.where(short_valid, short_scores, floor_score)
    short_top = jnp.max(short_scores, axis=-1, keepdims=True)
    short_expo = jnp.where(short_valid, jnp.exp(short_scores - short_top), 0.0)
    short_weights = (short_expo / jnp.sum(short_expo, axis=-1, keepdims=True)).astype(jnp.bfloat16)
    short_mix = jnp.einsum(
        "rkgs,rksd->rkgd",
        short_weights,
        short_out[..., head_size:],
        preferred_element_type=jnp.float32,
    )
    span = long_cache.shape[2]
    first_slot = lax.axis_index("req") * span
    long_slots = first_slot + jnp.arange(span, dtype=jnp.int32)
    long_write = long_slots[None, :] == long_lengths[:, None]
    long_out = jnp.where(long_write[:, None, :, None], fresh[short_count:, :, None, :], long_cache)
    long_scores = (
        jnp.einsum(
            "lkgd,lksd->lkgs",
            query[short_count:],
            long_out[..., :head_size],
            preferred_element_type=jnp.float32,
        )
        * score_scale
    )
    long_valid = (long_slots[None, :] <= long_lengths[:, None])[:, None, None, :]
    long_scores = jnp.where(long_valid, long_scores, floor_score)
    long_peak = jnp.max(long_scores, axis=-1)
    long_expo = jnp.where(long_valid, jnp.exp(long_scores - long_peak[..., None]), 0.0)
    long_total = jnp.sum(long_expo, axis=-1)
    long_summed = jnp.einsum(
        "lkgs,lksd->lkgd",
        long_expo,
        long_out[..., head_size:].astype(jnp.float32),
        precision=lax.Precision.HIGHEST,
    )
    peak_all, total_all, summed_all = merged(
        (long_peak, long_total, long_summed), "req", join_partials
    )
    long_mix = summed_all / total_all[..., None]
    mixed = jnp.concatenate(
        [short_mix.reshape(short_count, -1), long_mix.reshape(long_count, -1)], axis=0
    ).astype(jnp.bfloat16)
    head_terms = jnp.dot(mixed, w_out, preferred_element_type=jnp.float32)
    summed_heads = lax.psum(head_terms, "tp")
    hidden = (residual + summed_heads).astype(jnp.bfloat16)
    return (hidden[:short_count], hidden[short_count:], short_out, long_out)


def solution(mesh):
    placed = (
        P("req", None),
        P(),
        P(),
        P(None, "tp"),
        P(None, "tp"),
        P(None, "tp"),
        P("tp", None),
        P("req"),
        P(),
        P("req", "tp", None, None),
        P(None, "tp", "req", None),
    )
    return jax.shard_map(
        per_device,
        mesh=mesh,
        in_specs=placed,
        out_specs=(P("req", None), P(), P("req", "tp", None, None), P(None, "tp", "req", None)),
        check_vma=False,
    )
```

profile of v0, /device:TPU:0, one launch (start us, length us, event | category | flops | bytes accessed | tf_op | source)
XLA Modules:
  0.0 178.5 jit_solution(13294808918669247572)
XLA Ops:
  7.3 0.8 convert_element_type.43
  8.1 1.4 fusion.7
  9.5 0.7 iota_compare_fusion.1
  10.3 0.8 add_convert_fusion.1
  11.0 0.9 multiply_cosine_fusion.1
  11.9 1.9 %convolution_bitcast_fusion = f32[104,1,128]{2,0,1:T(8,128)S(1)} fusion(bf16[3072,128]{1,0:T(8,128)(2,1)} %param.17, f32[3072]{0:T(1024)S(1)} %convert_element_type.43, f32[104]{0:T(128)S(1)} %add_rsqrt_fusion, bf16[8,3072]{1,0:T(8,128)(2,1)} %param.14, bf16[96,3072]{1,0:T(8,128)(2,1)} %param.13), kind=kOutput, calls=%fused_computation.33 | convolution fusion | flops 84025344 | bytes 1491360 | tf_op jit(solution)/shard_map/dot_general | solution.py:75
  13.8 0.3 fusion.30
  14.1 0.4 fusion.18
  14.5 0.7 pad_maximum_fusion.2
  15.3 1.1 fusion.43
  16.5 0.1 copy.64
  16.6 0.1 copy.65
  16.7 0.7 broadcast_compare_fusion.1
  17.5 1.9 %bitcast_select_fusion.1 = bf16[8,1,512,256]{3,2,0,1:T(8,128)(2,1)S(1)} fusion(bf16[8,1,512,256]{3,2,1,0:T(8,128)(2,1)} %param.23, pred[8,512]{1,0:T(8,128)(4,1)S(1)} %get-tuple-element.102, bf16[8,256]{1,0:T(8,128)(2,1)S(1)} %maximum_bitcast_fusion), kind=kLoop, calls=%fused_computation.17 | loop fusion | flops 1048576 | bytes 4202496 | tf_op jit(solution)/shard_map/jit(_where)/select_n | solution.py:115
  19.4 0.1 subtract_convert_fusion
  19.6 0.5 fusion.47
  20.1 0.6 fusion.19
  20.7 25.5 %all-gather.2 = f32[128,3,128]{2,0,1:T(8,128)S(1)} all-gather(f32[8,3,128]{2,0,1:T(8,128)S(1)} %copy.51), channel_id=4, replica_groups=mesh['req'=16,'tp'=8] {'req'}, dimensions={0}, use_global_device_ids=true | all-gather | bytes 208896 | tf_op jit(solution)/shard_map/all_gather | solution.py:11
  46.2 0.2 fusion.33
  46.4 0.1 copy.50
  46.5 22.8 %all-gather.4 = f32[16,8,3]{1,2,0:T(4,128)S(1)} all-gather(f32[1,8,3]{1,2,0:T(4,128)S(1)} %bitcast.102), channel_id=3, replica_groups=mesh['req'=16,'tp'=8] {'req'}, dimensions={0}, use_global_device_ids=true | all-gather | bytes 1632 | tf_op jit(solution)/shard_map/all_gather | solution.py:11
  69.3 0.1 copy.49
  69.4 21.1 %all-gather.3 = f32[16,8,3]{1,2,0:T(4,128)S(1)} all-gather(f32[1,8,3]{1,2,0:T(4,128)S(1)} %bitcast.103), channel_id=2, replica_groups=mesh['req'=16,'tp'=8] {'req'}, dimensions={0}, use_global_device_ids=true | all-gather | bytes 1632 | tf_op jit(solution)/shard_map/all_gather | solution.py:11
  90.5 6.2 %bitcast_select_fusion = bf16[96,1,128,256]{3,2,0,1:T(8,128)(2,1)S(1)} fusion(bf16[96,1,128,256]{3,2,1,0:T(8,128)(2,1)} %param.22, pred[96,128]{1,0:T(8,128)(4,1)S(1)} %get-tuple-element.106, bf16[96,256]{1,0:T(8,128)(2,1)S(1)} %slice_bitcast_fusion.15), kind=kLoop, calls=%fused_computation.12 | loop fusion | flops 3145728 | bytes 12644352 | tf_op jit(solution)/shard_map/jit(_where)/select_n | solution.py:88
  96.7 1.8 fusion.15
  98.5 0.3 fusion.48
  98.8 1.0 fusion.16
  99.9 4.6 %while.14 = (s32[]{:T(128)}, f32[8,1,3]{0,1,2:T(1,128)S(1)}, f32[8,1,3]{0,1,2:T(1,128)S(1)}, f32[8,1,3,128]{3,2,1,0:T(4,128)S(1)}, f32[15,8,1,3]{1,0,3,2:T(8,128...) while((s32[]{:T(128)}, f32[8,1,3]{0,1,2:T(1,128)S(1)}, ...), condition=%wide.region_6.7_spmd, body=%wide.region_5.6_spmd.sunk | while | flops 9362 | bytes 62877 | solution.py:14
  100.0 0.1 copy.85
  100.1 0.1 fusion.59
  100.3 0.1 copy.85
  100.4 0.1 fusion.59
  100.6 0.1 copy.85
  100.7 0.1 fusion.59
  100.9 0.1 copy.85
  101.1 0.1 fusion.59
  101.2 0.1 copy.85
  101.4 0.1 fusion.59
  101.5 0.1 copy.85
  101.7 0.1 fusion.59
  101.8 0.1 copy.85
  102.0 0.1 fusion.59
  102.1 0.1 copy.85
  102.3 0.1 fusion.59
  102.4 0.1 copy.85
  102.6 0.1 fusion.59
  102.7 0.1 copy.85
  102.9 0.1 fusion.59
  103.0 0.1 copy.85
  103.2 0.1 fusion.59
  103.3 0.1 copy.85
  103.5 0.1 fusion.59
  103.8 0.1 fusion.59
  104.0 0.1 copy.85
  104.1 0.1 fusion.59
  104.3 0.1 copy.85
  104.4 0.1 fusion.59
  104.6 1.6 fusion.21
  106.2 2.9 %fusion.54 = bf16[8,1,512,256]{3,2,1,0:T(8,128)(2,1)} fusion(bf16[8,1,512,256]{3,2,1,0:T(8,128)(2,1)} %param.23, bf16[8,256]{1,0:T(8,128)(2,1)S(1)} %maximum_bitcast_fusion, pred[8,512]{1,0:T(8,128)(4,1)S(1)} %get-tuple-element.102), kind=kLoop, calls=%fused_computation.92 | loop fusion | flops 1048576 | bytes 4202496
  109.1 7.6 %fusion.55 = bf16[96,1,128,256]{3,2,1,0:T(8,128)(2,1)} fusion(bf16[96,1,128,256]{3,2,1,0:T(8,128)(2,1)} %param.22, bf16[96,256]{1,0:T(8,128)(2,1)S(1)} %slice_bitcast_fusion.15, pred[96,128]{1,0:T(8,128)(4,1)S(1)} %get-tuple-element.106), kind=kLoop, calls=%fused_computation.93 | loop fusion | flops 3145728 | bytes 12644352
  116.7 52.1 %all-reduce.2.cloned.1.call-done = f32[104,3072]{1,0:T(8,128)} async-done(((f32[104,3072]{1,0:T(8,128)}), f32[104,3072]{1,0:T(8,128)}) %all-reduce.2.cloned.1.call-update) | async-done | bytes 1277968 | tf_op jit(solution)/shard_map/psum | solution.py:144
  168.8 1.4 fusion.10
  170.2 0.9 slice.107
  171.1 0.6 slice.108
  (99 shorter events, 2.2 us)
Async XLA Ops:
  7.2 97.5 %copy-start = (bf16[384,3072]{1,0:T(8,128)(2,1)S(1)}, bf16[384,3072]{1,0:T(8,128)(2,1)}, u32[]{:S(2)}) copy-start(bf16[384,3072]{1,0:T(8,128)(2,1)} %param.19) | copy-start | bytes 7077892
  7.2 6.9 %copy-start.1 = (bf16[96,3072]{1,0:T(8,128)(2,1)S(1)}, bf16[96,3072]{1,0:T(8,128)(2,1)}, u32[]{:S(2)}) copy-start(bf16[96,3072]{1,0:T(8,128)(2,1)} %param.13) | copy-start | bytes 1769476
  7.2 6.9 %copy-start.4 = (bf16[8,3072]{1,0:T(8,128)(2,1)S(1)}, bf16[8,3072]{1,0:T(8,128)(2,1)}, u32[]{:S(2)}) copy-start(bf16[8,3072]{1,0:T(8,128)(2,1)} %param.14) | copy-start | bytes 147460
  7.2 161.6 %all-reduce.2.cloned.1.call-start = ((), (), s32[]{:S(2)}) async-start(), calls=%async_computation | async-start | bytes 2555904 | tf_op jit(solution)/shard_map/psum | solution.py:144
  7.2 6.9 %copy-start.13 = (bf16[3072,128]{1,0:T(8,128)(2,1)S(1)}, bf16[3072,128]{1,0:T(8,128)(2,1)}, u32[]{:S(2)}) copy-start(bf16[3072,128]{1,0:T(8,128)(2,1)} %param.18) | copy-start | bytes 2359300
  11.9 3.4 %copy-start.12 = (bf16[3072,384]{1,0:T(8,128)(2,1)S(1)}, bf16[3072,384]{1,0:T(8,128)(2,1)}, u32[]{:S(2)}) copy-start(bf16[3072,384]{1,0:T(8,128)(2,1)} %param.16) | copy-start | bytes 7077892
  17.5 2.0 %copy-start.2 = (f32[104,64]{1,0:T(8,128)S(1)}, f32[104,64]{1,0:T(8,128)}, u32[]{:S(2)}) copy-start(f32[104,64]{1,0:T(8,128)} %get-tuple-element.104) | copy-start | bytes 79876
  19.6 26.6 %copy-start.8 = (bf16[104,3,64]{2,1,0:T(4,128)(2,1)}, bf16[104,3,64]{2,1,0:T(4,128)(2,1)S(1)}, u32[]{:S(2)}) copy-start(bf16[104,3,64]{2,1,0:T(4,128)(2,1)S(1)} %get-tuple-element.95) | copy-start | bytes 119812
  19.6 26.6 %copy-start.10 = (bf16[104,3,64]{2,1,0:T(4,128)(2,1)}, bf16[104,3,64]{2,1,0:T(4,128)(2,1)S(1)}, u32[]{:S(2)}) copy-start(bf16[104,3,64]{2,1,0:T(4,128)(2,1)S(1)} %get-tuple-element.96) | copy-start | bytes 119812
  19.6 70.9 %copy-start.3 = (bf16[104,1,256]{2,0,1:T(8,128)(2,1)S(1)}, bf16[104,1,256]{2,0,1:T(8,128)(2,1)}, u32[]{:S(2)}) copy-start(bf16[104,1,256]{2,0,1:T(8,128)(2,1)} %pad_maximum_fusion.2) | copy-start | bytes 159748
  69.3 27.4 %copy-start.6 = (f32[16,8,3]{1,2,0:T(4,128)}, f32[16,8,3]{1,2,0:T(4,128)S(1)}, u32[]{:S(2)}) copy-start(f32[16,8,3]{1,2,0:T(4,128)S(1)} %all-gather.4) | copy-start | bytes 4612
  90.5 6.3 %copy-start.7 = (f32[16,8,3]{1,2,0:T(4,128)}, f32[16,8,3]{1,2,0:T(4,128)S(1)}, u32[]{:S(2)}) copy-start(f32[16,8,3]{1,2,0:T(4,128)S(1)} %all-gather.3) | copy-start | bytes 4612
  90.5 6.2 %copy-start.9 = (bf16[104,3,64]{2,1,0:T(4,128)(2,1)S(1)}, bf16[104,3,64]{2,1,0:T(4,128)(2,1)}, u32[]{:S(2)}) copy-start(bf16[104,3,64]{2,1,0:T(4,128)(2,1)} %copy-done.8) | copy-start | bytes 119812
  90.5 6.2 %copy-start.11 = (bf16[104,3,64]{2,1,0:T(4,128)(2,1)S(1)}, bf16[104,3,64]{2,1,0:T(4,128)(2,1)}, u32[]{:S(2)}) copy-start(bf16[104,3,64]{2,1,0:T(4,128)(2,1)} %copy-done.10) | copy-start | bytes 119812
  98.8 1.1 slice-start
  98.8 1.1 slice-start.1
  109.1 59.6 %copy-start.5 = (bf16[8,3072]{1,0:T(8,128)(2,1)S(1)}, bf16[8,3072]{1,0:T(8,128)(2,1)}, u32[]{:S(2)}) copy-start(bf16[8,3072]{1,0:T(8,128)(2,1)} %param.14) | copy-start | bytes 147460
Sparse Core Ops, SparseCore 0:
  106.3 62.3 all-reduce.1
where the time goes:
time: 179 us
  blocking collectives  69.3 us (39%)
  waiting for transfers between devices  52.1 us (29%)
  other arithmetic  29 us (16%)
  between operations  14.5 us (8%)
  matrix products  8.79 us (5%)
  local copies, waits for them, and re-layouts  4.56 us (3%)
    all_gather x3, blocking collectives, merged(): pieces = jax.tree.map(lambda part: lax.all_gather(part, axis), value)  69.3 us
    psum x1, waiting for transfers between devices, per_device(): summed_heads = lax.psum(head_terms, 'tp')  52.1 us
    unnamed x2, other arithmetic  10.5 us
    select_n x1, other arithmetic, per_device(): jnp.where(short_write[:, None, :, None], fresh[:short_count, :, None, :],...  6.17 us
  transfers between devices with their start and end apart: 1, of which 1 were waited for; matrix products, arithmetic and copies ran while one was open for 6% of the time, Pallas kernels for 0%

commit v1 on v0

--- a/solution.py
+++ b/solution.py
@@ -141,7 +141,11 @@
         [short_mix.reshape(short_count, -1), long_mix.reshape(long_count, -1)], axis=0
     ).astype(jnp.bfloat16)
     head_terms = jnp.dot(mixed, w_out, preferred_element_type=jnp.float32)
-    summed_heads = lax.psum(head_terms, "tp")
+    summed_heads = head_terms
+    for hop in (1, 2, 4):
+        summed_heads = summed_heads + lax.ppermute(
+            summed_heads, "tp", [(dev, dev ^ hop) for dev in range(8)]
+        )
     hidden = (residual + summed_heads).astype(jnp.bfloat16)
     return (hidden[:short_count], hidden[short_count:], short_out, long_out)
 

time: 179 us -> 166 us (0.927)
  between operations: 14.5 us -> 1.09 us
  other arithmetic: 29 us -> 23.5 us
  starting transfers between devices: 0.04 us -> 4.76 us
    ppermute x0 -> x3, waiting for transfers between devices: none -> 53.4 us  [per_device(): lax.ppermute(summed_heads, 'tp', [(dev, dev ^ hop) for dev in range(8)])]
    psum x1 -> x0, waiting for transfers between devices: 52.1 us -> none  [per_device(): summed_heads = lax.psum(head_terms, 'tp')]
    ppermute x0 -> x3, starting transfers between devices: none -> 4.76 us  [per_device(): lax.ppermute(summed_heads, 'tp', [(dev, dev ^ hop) for dev in range(8)])]
    unnamed x2 -> x3, other arithmetic: 10.5 us -> 5.97 us
  transfers between devices with their start and end apart: 1 -> 3, of which waited for: 1 -> 3; matrix products, arithmetic and copies ran while one was open for 6% -> 4% of each run, Pallas kernels for 0% -> 0%
where the time goes in v1:
time: 166 us; the launch traced here: 165 us
  blocking collectives  69.3 us (42%)
  waiting for transfers between devices  53.4 us (32%)
  other arithmetic  23.5 us (14%)
  matrix products  7.72 us (5%)
  local copies, waits for them, and re-layouts  5.02 us (3%)
  starting transfers between devices  4.76 us (3%)
    all_gather x3, blocking collectives, merged(): pieces = jax.tree.map(lambda part: lax.all_gather(part, axis), value)  69.3 us
    ppermute x3, waiting for transfers between devices, per_device(): lax.ppermute(summed_heads, 'tp', [(dev, dev ^ hop) for dev in range(8)])  53.4 us
    select_n x1, other arithmetic, per_device(): jnp.where(short_write[:, None, :, None], fresh[:short_count, :, None, :],...  6.17 us
    unnamed x3, other arithmetic  5.97 us
    ppermute x3, starting transfers between devices, per_device(): lax.ppermute(summed_heads, 'tp', [(dev, dev ^ hop) for dev in range(8)])  4.76 us
  transfers between devices with their start and end apart: 3, of which 3 were waited for; matrix products, arithmetic and copies ran while one was open for 4% of the time, Pallas kernels for 0%

profile of v1, /device:TPU:0, one launch (start us, length us, event | category | flops | bytes accessed | tf_op | source)
XLA Modules:
  0.0 165.0 jit_solution(15543542011339521063)
XLA Ops:
  0.7 0.8 convert_element_type.43
  1.5 1.3 fusion.7
  2.8 0.7 iota_compare_fusion.1
  3.6 0.8 add_convert_fusion.1
  4.3 0.9 multiply_cosine_fusion.1
  5.2 1.8 %convolution_bitcast_fusion = f32[104,1,128]{2,0,1:T(8,128)S(1)} fusion(bf16[3072,128]{1,0:T(8,128)(2,1)} %param.17, f32[3072]{0:T(1024)S(1)} %convert_element_type.43, f32[104]{0:T(128)S(1)} %add_rsqrt_fusion, bf16[8,3072]{1,0:T(8,128)(2,1)} %param.14, bf16[96,3072]{1,0:T(8,128)(2,1)} %param.13), kind=kOutput, calls=%fused_computation.33 | convolution fusion | flops 84025344 | bytes 1491360 | tf_op jit(solution)/shard_map/dot_general | solution.py:75
  7.1 0.3 fusion.30
  7.4 0.4 fusion.18
  7.8 0.7 pad_maximum_fusion.2
  8.6 0.5 copy-done.13
  9.1 1.1 fusion.43
  10.2 0.1 copy.64
  10.4 0.1 copy.65
  10.5 0.7 broadcast_compare_fusion.1
  11.2 1.9 %bitcast_select_fusion.1 = bf16[8,1,512,256]{3,2,0,1:T(8,128)(2,1)S(1)} fusion(bf16[8,1,512,256]{3,2,1,0:T(8,128)(2,1)} %param.23, pred[8,512]{1,0:T(8,128)(4,1)S(1)} %get-tuple-element.102, bf16[8,256]{1,0:T(8,128)(2,1)S(1)} %maximum_bitcast_fusion), kind=kLoop, calls=%fused_computation.17 | loop fusion | flops 1048576 | bytes 4202496 | tf_op jit(solution)/shard_map/jit(_where)/select_n | solution.py:115
  13.2 0.1 subtract_convert_fusion
  13.4 0.5 fusion.47
  13.8 0.6 fusion.19
  14.5 25.5 %all-gather.2 = f32[128,3,128]{2,0,1:T(8,128)S(1)} all-gather(f32[8,3,128]{2,0,1:T(8,128)S(1)} %copy.51), channel_id=4, replica_groups=mesh['req'=16,'tp'=8] {'req'}, dimensions={0}, use_global_device_ids=true | all-gather | bytes 208896 | tf_op jit(solution)/shard_map/all_gather | solution.py:11
  40.0 0.2 fusion.33
  40.2 0.1 copy.50
  40.2 22.8 %all-gather.4 = f32[16,8,3]{1,2,0:T(4,128)S(1)} all-gather(f32[1,8,3]{1,2,0:T(4,128)S(1)} %bitcast.104), channel_id=3, replica_groups=mesh['req'=16,'tp'=8] {'req'}, dimensions={0}, use_global_device_ids=true | all-gather | bytes 1632 | tf_op jit(solution)/shard_map/all_gather | solution.py:11
  63.1 0.1 copy.49
  63.2 21.1 %all-gather.3 = f32[16,8,3]{1,2,0:T(4,128)S(1)} all-gather(f32[1,8,3]{1,2,0:T(4,128)S(1)} %bitcast.105), channel_id=2, replica_groups=mesh['req'=16,'tp'=8] {'req'}, dimensions={0}, use_global_device_ids=true | all-gather | bytes 1632 | tf_op jit(solution)/shard_map/all_gather | solution.py:11
  84.3 6.2 %bitcast_select_fusion = bf16[96,1,128,256]{3,2,0,1:T(8,128)(2,1)S(1)} fusion(bf16[96,1,128,256]{3,2,1,0:T(8,128)(2,1)} %param.22, pred[96,128]{1,0:T(8,128)(4,1)S(1)} %get-tuple-element.106, bf16[96,256]{1,0:T(8,128)(2,1)S(1)} %slice_bitcast_fusion.15), kind=kLoop, calls=%fused_computation.12 | loop fusion | flops 3145728 | bytes 12644352 | tf_op jit(solution)/shard_map/jit(_where)/select_n | solution.py:88
  90.5 1.8 %fusion.15 = f32[96,3,128]{2,1,0:T(4,128)S(1)} fusion(bf16[96,1,128,256]{3,2,0,1:T(8,128)(2,1)S(1)} %bitcast_select_fusion, pred[96,128]{1,0:T(8,128)(4,1)S(1)} %get-tuple-element.105, bf16[104,3,64]{2,1,0:T(4,128)(2,1)S(1)} %copy-done.12, bf16[104,3,64]{2,1,0:T(4,128)(2,1)S(1)} %copy-done.10), kind=kOutput, calls=%fused_computation.29 | convolution fusion | flops 9670656 | bytes 3518464 | tf_op jit(solution)/shard_map/rkgd,rksd->rkgs/dot_general | solution.py:92
  92.3 0.3 fusion.48
  92.6 1.0 fusion.16
  93.7 4.6 %while.14 = (s32[]{:T(128)}, f32[8,1,3]{0,1,2:T(1,128)S(1)}, f32[8,1,3]{0,1,2:T(1,128)S(1)}, f32[8,1,3,128]{3,2,1,0:T(4,128)S(1)}, f32[15,8,1,3]{1,0,3,2:T(8,128...) while((s32[]{:T(128)}, f32[8,1,3]{0,1,2:T(1,128)S(1)}, ...), condition=%wide.region_6.7_spmd, body=%wide.region_5.6_spmd.sunk | while | flops 9362 | bytes 62877 | solution.py:14
  93.7 0.1 copy.85
  93.9 0.1 fusion.59
  94.0 0.1 copy.85
  94.2 0.1 fusion.59
  94.3 0.1 copy.85
  94.5 0.1 fusion.59
  94.6 0.1 copy.85
  94.8 0.1 fusion.59
  94.9 0.1 copy.85
  95.1 0.1 fusion.59
  95.3 0.1 copy.85
  95.4 0.1 fusion.59
  95.7 0.1 fusion.59
  96.0 0.1 fusion.59
  96.3 0.1 fusion.59
  96.6 0.1 fusion.59
  97.0 0.1 fusion.59
  97.3 0.1 fusion.59
  97.6 0.1 fusion.59
  97.9 0.1 fusion.59
  98.2 0.1 fusion.59
  98.4 0.5 fusion.21
  98.9 0.1 collective-permute-start
  99.0 3.0 %collective-permute-done = f32[104,3072]{1,0:T(8,128)S(1)} collective-permute-done((f32[104,3072]{1,0:T(8,128)S(1)}, f32[104,3072]{1,0:T(8,128)S(1)}, u32[]{:S(2)}, u32[]{:S(2)}) %collective-permute-start) | collective-permute-done | bytes 1277984 | tf_op jit(solution)/shard_map/ppermute | solution.py:146
  102.0 0.1 add.54
  102.1 1.6 collective-permute-start.1
  103.7 28.6 %collective-permute-done.1 = f32[104,3072]{1,0:T(8,128)S(1)} collective-permute-done((f32[104,3072]{1,0:T(8,128)S(1)}, f32[104,3072]{1,0:T(8,128)S(1)}, u32[]{:S(2)}, u32[]{:S(2)}) %collective-permute-start.1) | collective-permute-done | bytes 1277984 | tf_op jit(solution)/shard_map/ppermute | solution.py:146
  132.3 0.1 add.55
  132.5 3.1 %collective-permute-start.2 = (f32[104,3072]{1,0:T(8,128)S(1)}, f32[104,3072]{1,0:T(8,128)S(1)}, u32[]{:S(2)}, u32[]{:S(2)}) collective-permute-start(f32[104,3072]{1,0:T(8,128)S(1)} %add.55), channel_id=1, source_target_pairs={{0,4},{1,5},{2,6},{3,7},{4,0},{5,1},{6,2},{7,3},{8,12},{9,13},{10,... | collective-permute-start | bytes 3833864 | tf_op jit(solution)/shard_map/ppermute | solution.py:146
  135.6 1.7 %fusion.54 = bf16[8,1,512,256]{3,2,1,0:T(8,128)(2,1)} fusion(bf16[8,1,512,256]{3,2,1,0:T(8,128)(2,1)S(1)} %copy-done.1, bf16[8,256]{1,0:T(8,128)(2,1)S(1)} %maximum_bitcast_fusion, pred[8,512]{1,0:T(8,128)(4,1)S(1)} %get-tuple-element.102), kind=kLoop, calls=%fused_computation.92 | loop fusion | flops 1048576 | bytes 4202496
  137.3 4.3 %fusion.55 = bf16[96,1,128,256]{3,2,1,0:T(8,128)(2,1)} fusion(bf16[96,1,128,256]{3,2,1,0:T(8,128)(2,1)S(1)} %bitcast.97, bf16[96,256]{1,0:T(8,128)(2,1)S(1)} %slice_bitcast_fusion.15, pred[96,128]{1,0:T(8,128)(4,1)S(1)} %get-tuple-element.106), kind=kLoop, calls=%fused_computation.93 | loop fusion | flops 3145728 | bytes 12644352
  141.6 21.8 %collective-permute-done.2 = f32[104,3072]{1,0:T(8,128)S(1)} collective-permute-done((f32[104,3072]{1,0:T(8,128)S(1)}, f32[104,3072]{1,0:T(8,128)S(1)}, u32[]{:S(2)}, u32[]{:S(2)}) %collective-permute-start.2) | collective-permute-done | bytes 1277984 | tf_op jit(solution)/shard_map/ppermute | solution.py:146
  163.3 0.2 fusion.10
  163.6 0.9 slice.107
  164.4 0.6 slice.108
  (111 shorter events, 2.8 us)
Async XLA Ops:
  0.6 97.7 %copy-start = (bf16[384,3072]{1,0:T(8,128)(2,1)S(1)}, bf16[384,3072]{1,0:T(8,128)(2,1)}, u32[]{:S(2)}) copy-start(bf16[384,3072]{1,0:T(8,128)(2,1)} %param.19) | copy-start | bytes 7077892
  5.2 2.1 %copy-start.2 = (bf16[96,3072]{1,0:T(8,128)(2,1)S(1)}, bf16[96,3072]{1,0:T(8,128)(2,1)}, u32[]{:S(2)}) copy-start(bf16[96,3072]{1,0:T(8,128)(2,1)} %param.13) | copy-start | bytes 1769476
  5.2 2.1 %copy-start.5 = (bf16[8,3072]{1,0:T(8,128)(2,1)S(1)}, bf16[8,3072]{1,0:T(8,128)(2,1)}, u32[]{:S(2)}) copy-start(bf16[8,3072]{1,0:T(8,128)(2,1)} %param.14) | copy-start | bytes 147460
  5.2 2.1 %copy-start.14 = (bf16[3072,128]{1,0:T(8,128)(2,1)S(1)}, bf16[3072,128]{1,0:T(8,128)(2,1)}, u32[]{:S(2)}) copy-start(bf16[3072,128]{1,0:T(8,128)(2,1)} %param.18) | copy-start | bytes 2359300
  7.4 1.7 %copy-start.13 = (bf16[3072,384]{1,0:T(8,128)(2,1)S(1)}, bf16[3072,384]{1,0:T(8,128)(2,1)}, u32[]{:S(2)}) copy-start(bf16[3072,384]{1,0:T(8,128)(2,1)} %param.16) | copy-start | bytes 7077892
  11.2 2.0 %copy-start.3 = (f32[104,64]{1,0:T(8,128)S(1)}, f32[104,64]{1,0:T(8,128)}, u32[]{:S(2)}) copy-start(f32[104,64]{1,0:T(8,128)} %get-tuple-element.104) | copy-start | bytes 79876
  13.3 1.1 copy-start.9
  13.3 1.1 copy-start.11
  13.8 70.4 %copy-start.4 = (bf16[104,1,256]{2,0,1:T(8,128)(2,1)S(1)}, bf16[104,1,256]{2,0,1:T(8,128)(2,1)}, u32[]{:S(2)}) copy-start(bf16[104,1,256]{2,0,1:T(8,128)(2,1)} %pad_maximum_fusion.2) | copy-start | bytes 159748
  63.0 27.4 %copy-start.7 = (f32[16,8,3]{1,2,0:T(4,128)}, f32[16,8,3]{1,2,0:T(4,128)S(1)}, u32[]{:S(2)}) copy-start(f32[16,8,3]{1,2,0:T(4,128)S(1)} %all-gather.4) | copy-start | bytes 4612
  84.2 6.3 %copy-start.8 = (f32[16,8,3]{1,2,0:T(4,128)}, f32[16,8,3]{1,2,0:T(4,128)S(1)}, u32[]{:S(2)}) copy-start(f32[16,8,3]{1,2,0:T(4,128)S(1)} %all-gather.3) | copy-start | bytes 4612
  84.3 6.2 %copy-start.10 = (bf16[104,3,64]{2,1,0:T(4,128)(2,1)S(1)}, bf16[104,3,64]{2,1,0:T(4,128)(2,1)}, u32[]{:S(2)}) copy-start(bf16[104,3,64]{2,1,0:T(4,128)(2,1)} %copy-done.9) | copy-start | bytes 119812
  84.3 6.2 %copy-start.12 = (bf16[104,3,64]{2,1,0:T(4,128)(2,1)S(1)}, bf16[104,3,64]{2,1,0:T(4,128)(2,1)}, u32[]{:S(2)}) copy-start(bf16[104,3,64]{2,1,0:T(4,128)(2,1)} %copy-done.11) | copy-start | bytes 119812
  92.6 1.1 slice-start.2
  92.6 1.1 slice-start.3
  98.9 3.1 %collective-permute-start = (f32[104,3072]{1,0:T(8,128)S(1)}, f32[104,3072]{1,0:T(8,128)S(1)}, u32[]{:S(2)}, u32[]{:S(2)}) collective-permute-start(f32[104,3072]{1,0:T(8,128)S(1)} %fusion.21), channel_id=1, source_target_pairs={{0,1},{1,0},{2,3},{3,2},{4,5},{5,4},{6,7},{7,6},{8,9},{9,8},{10,11... | collective-permute-start | bytes 3833864 | tf_op jit(solution)/shard_map/ppermute | solution.py:146
  102.0 33.6 %copy-start.1 = (bf16[8,1,512,256]{3,2,1,0:T(8,128)(2,1)S(1)}, bf16[8,1,512,256]{3,2,1,0:T(8,128)(2,1)}, u32[]{:S(2)}) copy-start(bf16[8,1,512,256]{3,2,1,0:T(8,128)(2,1)} %param.23) | copy-start | bytes 6291460
  102.0 35.3 %slice-start = ((s8[6291456]{0:T(1024)(128)(4,1)}), s8[4194304]{0:T(1024)(128)(4,1)S(1)}, s32[]{:S(2)}) async-start(s8[6291456]{0:T(1024)(128)(4,1)} %bitcast.96), calls=%async_computation | async-start | bytes 8388608
  102.1 35.1 %slice-start.1 = ((s8[6291456]{0:T(1024)(128)(4,1)}), s8[2097152]{0:T(1024)(128)(4,1)S(1)}, s32[]{:S(2)}) async-start(s8[6291456]{0:T(1024)(128)(4,1)} %bitcast.96), calls=%async_computation.1 | async-start | bytes 4194304
  102.1 30.2 %collective-permute-start.1 = (f32[104,3072]{1,0:T(8,128)S(1)}, f32[104,3072]{1,0:T(8,128)S(1)}, u32[]{:S(2)}, u32[]{:S(2)}) collective-permute-start(f32[104,3072]{1,0:T(8,128)S(1)} %add.54), channel_id=1, source_target_pairs={{0,2},{1,3},{2,0},{3,1},{4,6},{5,7},{6,4},{7,5},{8,10},{9,11},{10,... | collective-permute-start | bytes 3833864 | tf_op jit(solution)/shard_map/ppermute | solution.py:146
  132.5 30.8 %collective-permute-start.2 = (f32[104,3072]{1,0:T(8,128)S(1)}, f32[104,3072]{1,0:T(8,128)S(1)}, u32[]{:S(2)}, u32[]{:S(2)}) collective-permute-start(f32[104,3072]{1,0:T(8,128)S(1)} %add.55), channel_id=1, source_target_pairs={{0,4},{1,5},{2,6},{3,7},{4,0},{5,1},{6,2},{7,3},{8,12},{9,13},{10,... | collective-permute-start | bytes 3833864 | tf_op jit(solution)/shard_map/ppermute | solution.py:146
  137.3 26.1 %copy-start.6 = (bf16[8,3072]{1,0:T(8,128)(2,1)S(1)}, bf16[8,3072]{1,0:T(8,128)(2,1)}, u32[]{:S(2)}) copy-start(bf16[8,3072]{1,0:T(8,128)(2,1)} %param.14) | copy-start | bytes 147460
